TPU v7x, 256 devices: a whole 4x4x8 slice. The times are simulated.
256 devices in a mesh: row: 16 (over z_hi, y, core), col: 16 (over z_lo, x).
Axes of the slice: x: 4, y: 4, z: 8 (z_hi: 2, z_lo: 4; z = z_hi * 4 + z_lo), core: 2. Of those that a mesh axis runs over, the one named last changes fastest.
Arguments:
- features: bfloat16 [65536, 128], P(('col', 'row')), may hold values from -6 to 6
- weight: bfloat16 [128, 128], replicated, may hold values from -0.5 to 0.5
- tiles: bfloat16 [16, 16, 352, 128, 128], P('row', 'col'), may hold values from -0.0546875 to 0.0546875
- tile_slots: int32 [16, 16, 352], P('row', 'col'), may hold values from 0 to 1023, as said below
- tile_counts: int32 [16, 16], P('row', 'col'), may hold values from 44 to 352, as said below
- cotangent: bfloat16 [65536, 128], P(('row', 'col')), may hold values from -6 to 6
Outputs:
- hidden: bfloat16 [65536, 128], P(('row', 'col'))
- feature_grad: bfloat16 [65536, 128], P(('col', 'row'))
- weight_grad: float32 [128, 128], replicated
Inputs may be any that keep to these rules, and one draw needn't show every extreme that they name: `tile_slots`: the slots of one block are distinct. `tile_counts`: some block has all 352 slots live.
All inputs are finite; a program needn't handle non-finite values.
Results may differ from a plain program's by a relative error of at most 0.006.
Values may be sent and summed in bfloat16 or wider, within the bound.
A program may use at most 128 MiB of HBM per device.

v0:
```python
import math
import jax
import jax.numpy as jnp
from jax import lax
from jax.sharding import PartitionSpec as P


def silu_grad(values):
    sig = jax.nn.sigmoid(values)
    return sig * (1.0 + values * (1.0 - sig))


def body(features, weight, tiles, tile_slots, tile_counts, cotangent):
    tile_vals = tiles[0, 0]
    slot_ids = tile_slots[0, 0]
    live_count = tile_counts[0, 0]
    tile_size = tile_vals.shape[-1]
    share_rows = features.shape[0]
    width = features.shape[1]
    slot_total = slot_ids.shape[0]
    row_count = lax.axis_size("row")
    col_count = lax.axis_size("col")
    tile_rows = share_rows * col_count // tile_size
    tile_cols = share_rows * row_count // tile_size
    col_index = lax.axis_index("col")
    projected = jnp.dot(features, weight, preferred_element_type=jnp.float32).astype(jnp.bfloat16)
    proj_block = lax.all_gather(projected, "row", axis=0, tiled=True)
    is_live = jnp.arange(slot_total, dtype=jnp.int32) < live_count
    gathered = proj_block.reshape(tile_cols, tile_size, width)[slot_ids % tile_cols]
    products = jnp.einsum("tij,tjf->tif", tile_vals, gathered, preferred_element_type=jnp.float32)
    fwd_targets = jnp.where(is_live, slot_ids // tile_cols, tile_rows)
    partial_value = jax.ops.segment_sum(products, fwd_targets, tile_rows + 1)[:tile_rows].reshape(
        tile_rows * tile_size, width
    )
    summed = lax.psum(partial_value, "col")
    own_rows = lax.dynamic_slice_in_dim(summed, col_index * share_rows, share_rows, 0)
    hidden = jax.nn.silu(own_rows).astype(jnp.bfloat16)
    cot_block = lax.all_gather(cotangent, "col", axis=0, tiled=True)
    grad_block = (cot_block.astype(jnp.float32) * silu_grad(summed)).astype(jnp.bfloat16)
    grad_tiles = grad_block.reshape(tile_rows, tile_size, width)[slot_ids // tile_cols]
    back_products = jnp.einsum(
        "tji,tjf->tif", tile_vals, grad_tiles, preferred_element_type=jnp.float32
    )
    back_targets = jnp.where(is_live, slot_ids % tile_cols, tile_cols)
    back_partial = jax.ops.segment_sum(back_products, back_targets, tile_cols + 1)[
        :tile_cols
    ].reshape(tile_cols * tile_size, width)
    grad_proj = lax.psum_scatter(back_partial, "row", scatter_dimension=0, tiled=True).astype(
        jnp.bfloat16
    )
    feature_grad = jnp.dot(grad_proj, weight.T, preferred_element_type=jnp.float32).astype(
        jnp.bfloat16
    )
    weight_term = jnp.dot(features.T, grad_proj, preferred_element_type=jnp.float32)
    node_total = share_rows * row_count * col_count
    weight_grad = lax.psum(weight_term, ("row", "col")) / math.sqrt(node_total)
    return (hidden, feature_grad, weight_grad)


def solution(mesh):
    placed = (
        P(("col", "row"), None),
        P(),
        P("row", "col", None, None, None),
        P("row", "col", None),
        P("row", "col"),
        P(("row", "col"), None),
    )
    return jax.shard_map(
        body,
        mesh=mesh,
        in_specs=placed,
        out_specs=(P(("row", "col"), None), P(("col", "row"), None), P()),
        check_vma=False,
    )
```

profile of v0, /device:TPU:1, one launch (start us, length us, event | category | flops | bytes accessed | tf_op | source)
XLA Modules:
  0.0 771.6 jit_solution(9133756063964806921)
XLA Ops:
  7.2 0.8 copy-done
  8.0 1.5 convolution_convert_fusion.1
  11.0 0.7 fusion.15
  11.7 0.7 fusion.13
  12.4 58.8 %all-gather.3.cloned.1.call-done = bf16[4096,128]{1,0:T(8,128)(2,1)} async-done(((bf16[256,128]{1,0:T(8,128)(2,1)}), bf16[4096,128]{1,0:T(8,128)(2,1)}) %all-gather.3.cloned.1.call-update) | async-done | bytes 1048592 | tf_op jit(solution)/shard_map/all_gather | solution.py:27
  71.3 12.2 %gather_fusion = bf16[352,128,128]{2,1,0:T(8,128)(2,1)} fusion(bf16[32,128,128]{2,1,0:T(8,128)(2,1)} %bitcast.41, s32[1024]{0:T(1024)S(1)} %pad_clamp_fusion.1), kind=kCustom, calls=%fused_computation | custom fusion | bytes 23070080 | tf_op jit(solution)/shard_map/gather | solution.py:29
  83.5 20.6 %fusion.4 = f32[352,128,128]{1,2,0:T(8,128)} fusion(bf16[352,128,128]{2,1,0:T(8,128)(2,1)} %gather_fusion, bf16[1,1,352,128,128]{4,3,2,1,0:T(8,128)(2,1)} %param.8), kind=kOutput, calls=%fused_computation.8 | convolution fusion | flops 1476395008 | bytes 46137344 | tf_op jit(solution)/shard_map/tij,tjf->tif/dot_general | solution.py:30
  104.1 23.5 %copy.13 = f32[352,128,128]{2,1,0:T(8,128)} copy(f32[352,128,128]{1,2,0:T(8,128)} %fusion.4) | data formatting | bytes 46137344 | tf_op jit(solution)/shard_map/tij,tjf->tif/dot_general | solution.py:30
  127.8 46.0 %scatter_fusion = f32[33,128,128]{2,1,0:T(8,128)S(1)} fusion(f32[33,128,128]{2,1,0:T(8,128)S(1)} %broadcast.191.clone, s32[352]{0:T(512)S(1)} %get-tuple-element.10, f32[352,128,128]{2,1,0:T(8,128)} %copy.13), kind=kCustom, calls=%fused_computation.2 | custom fusion | flops 5767168 | bytes 69207424 | tf_op jit(solution)/shard_map/scatter-add | solution.py:32
  173.9 1.5 slice.12
  175.7 153.0 %all-reduce.3.cloned.1.call-done = f32[4096,128]{1,0:T(8,128)} async-done(((f32[4096,128]{1,0:T(8,128)}), f32[4096,128]{1,0:T(8,128)}) %all-reduce.3.cloned.1.call-update) | async-done | bytes 2097168 | tf_op jit(solution)/shard_map/psum | solution.py:35
  328.6 2.6 multiply_convert_fusion
  331.3 11.0 %gather_fusion.1 = bf16[352,128,128]{2,1,0:T(8,128)(2,1)} fusion(bf16[32,128,128]{2,1,0:T(8,128)(2,1)S(1)} %bitcast.40, s32[1024]{0:T(1024)S(1)} %pad_clamp_fusion), kind=kCustom, calls=%fused_computation.1 | custom fusion | bytes 23070080 | tf_op jit(solution)/shard_map/gather | solution.py:40
  342.3 14.4 %fusion.7 = f32[352,128,128]{1,2,0:T(8,128)} fusion(bf16[352,128,128]{2,1,0:T(8,128)(2,1)} %gather_fusion.1, bf16[1,1,352,128,128]{4,3,2,1,0:T(8,128)(2,1)} %param.8), kind=kOutput, calls=%fused_computation.9 | convolution fusion | flops 1476395008 | bytes 46137344 | tf_op jit(solution)/shard_map/tji,tjf->tif/dot_general | solution.py:41
  356.7 23.5 %copy.15 = f32[352,128,128]{2,1,0:T(8,128)} copy(f32[352,128,128]{1,2,0:T(8,128)} %fusion.7) | data formatting | bytes 46137344 | tf_op jit(solution)/shard_map/tji,tjf->tif/dot_general | solution.py:41
  380.4 46.0 %scatter_fusion.1 = f32[33,128,128]{2,1,0:T(8,128)S(1)} fusion(f32[33,128,128]{2,1,0:T(8,128)S(1)} %broadcast.191, s32[352]{0:T(512)S(1)} %get-tuple-element.11, f32[352,128,128]{2,1,0:T(8,128)} %copy.15), kind=kCustom, calls=%fused_computation.3 | custom fusion | flops 5767168 | bytes 69207424 | tf_op jit(solution)/shard_map/scatter-add | solution.py:45
  426.4 1.5 slice.13
  428.0 1.6 multiply_convert_fusion.1
  429.6 92.6 %reduce-scatter.2.cloned.1.call-done = f32[256,128]{1,0:T(8,128)} async-done(((f32[4096,128]{1,0:T(8,128)}), f32[256,128]{1,0:T(8,128)}) %reduce-scatter.2.cloned.1.call-update) | async-done | bytes 131088 | tf_op jit(solution)/shard_map/reduce_scatter | solution.py:48
  522.2 1.7 convolution_bitcast_fusion
  524.0 1.7 convolution_convert_fusion
  525.7 237.9 %all-reduce.5.cloned.1.call-done = f32[128,128]{0,1:T(8,128)} async-done(((f32[128,128]{0,1:T(8,128)}), f32[128,128]{0,1:T(8,128)}) %all-reduce.5.cloned.1.call-update) | async-done | bytes 65552 | tf_op jit(solution)/shard_map/psum | solution.py:56
  763.5 0.8 broadcast_multiply_fusion
  764.4 0.7 copy.16
  (18 shorter events, 1.7 us)
Async XLA Ops:
  7.2 0.8 copy-start
  7.2 64.1 %all-gather.3.cloned.1.call-start = ((), (), s32[]{:S(2)}) async-start(), calls=%async_computation.1 | async-start | bytes 1114112 | tf_op jit(solution)/shard_map/all_gather | solution.py:27
  9.6 166.1 %all-gather.5.cloned.1.call-start = ((), (), s32[]{:S(2)}) async-start(), calls=%async_computation.3 | async-start | bytes 1114112 | tf_op jit(solution)/shard_map/all_gather | solution.py:38
  10.3 318.3 %all-reduce.3.cloned.1.call-start = ((), (), s32[]{:S(2)}) async-start(), calls=%async_computation.2 | async-start | bytes 4194304 | tf_op jit(solution)/shard_map/psum | solution.py:35
  175.4 346.8 %reduce-scatter.2.cloned.1.call-start = ((), (), s32[]{:S(2)}) async-start(), calls=%async_computation.4 | async-start | bytes 2228224 | tf_op jit(solution)/shard_map/reduce_scatter | solution.py:48
  380.4 143.5 %copy-start.1 = (bf16[128,128]{1,0:T(8,128)(2,1)S(1)}, bf16[128,128]{1,0:T(8,128)(2,1)}, u32[]{:S(2)}) copy-start(bf16[128,128]{1,0:T(8,128)(2,1)} %param.7) | copy-start | bytes 98308
  428.0 335.5 %all-reduce.5.cloned.1.call-start = ((), (), s32[]{:S(2)}) async-start(), calls=%async_computation.5 | async-start | bytes 131072 | tf_op jit(solution)/shard_map/psum | solution.py:56
Sparse Core Ops, SparseCore 0:
  11.3 59.9 all-gather.2
  73.1 65.9 all-gather.4
  175.5 153.0 all-reduce.2
  428.1 94.0 reduce-scatter.1
  528.1 235.3 all-reduce.4
where the time goes:
time: 774 us; the launch traced here: 772 us
  waiting for transfers between devices  543 us (70%)
  other arithmetic  98.5 us (13%)
  local copies, waits for them, and re-layouts  75.1 us (10%)
  matrix products  40 us (5%)
  between operations  14.5 us (2%)
    psum x1, waiting for transfers between devices, body(): weight_grad = lax.psum(weight_term, ('row', 'col')) / math.sqrt(node_total)  238 us
    psum x1, waiting for transfers between devices, body(): summed = lax.psum(partial_value, 'col')  153 us
    reduce_scatter x1, waiting for transfers between devices, body(): lax.psum_scatter(back_partial, 'row', scatter_dimension=0, tiled=True)  92.6 us
    all_gather x1, waiting for transfers between devices, body(): proj_block = lax.all_gather(projected, 'row', axis=0, tiled=True)  58.8 us
    scatter-add x1, other arithmetic, body(): jax.ops.segment_sum(products, fwd_targets, tile_rows + 1)[:tile_rows]  46 us
    scatter-add x1, other arithmetic, body(): jax.ops.segment_sum(back_products, back_targets, tile_cols + 1)[:tile_cols]  46 us
    dot_general x1, local copies, waits for them, and re-layouts, body(): jnp.einsum('tij,tjf->tif', tile_vals, gathered, preferred_element_type=jn...  23.5 us
    dot_general x1, local copies, waits for them, and re-layouts, body(): jnp.einsum('tji,tjf->tif', tile_vals, grad_tiles, preferred_element_type=...  23.5 us
  transfers between devices with their start and end apart: 5, of which 4 were waited for; matrix products, arithmetic and copies ran while one was open for 14% of the time, Pallas kernels for 0%

commit v1 on v0

--- a/solution.py
+++ b/solution.py
@@ -3,6 +3,11 @@
 import jax.numpy as jnp
 from jax import lax
 from jax.sharding import PartitionSpec as P
+
+
+def axis_by_axis(array, one, other):
+    half = lax.psum(array, one)
+    return lax.psum(half, other)
 
 
 def silu_grad(values):
@@ -53,7 +58,7 @@
     )
     weight_term = jnp.dot(features.T, grad_proj, preferred_element_type=jnp.float32)
     node_total = share_rows * row_count * col_count
-    weight_grad = lax.psum(weight_term, ("row", "col")) / math.sqrt(node_total)
+    weight_grad = axis_by_axis(weight_term, "row", "col") / math.sqrt(node_total)
     return (hidden, feature_grad, weight_grad)
 
 

time: 774 us -> 847 us (1.094)
  waiting for transfers between devices: 543 us -> 609 us
    psum x1 -> x2, waiting for transfers between devices: 238 us -> 302 us  [the longest x1 161 us: axis_by_axis(): half = lax.psum(array, one)]
  transfers between devices with their start and end apart: 5 -> 6, of which waited for: 4 -> 5; matrix products, arithmetic and copies ran while one was open for 14% -> 13% of each run, Pallas kernels for 0% -> 0%
where the time goes in v1:
time: 847 us; the launch traced here: 838 us
  waiting for transfers between devices  609 us (72%)
  other arithmetic  98.5 us (12%)
  local copies, waits for them, and re-layouts  75.1 us (9%)
  matrix products  40 us (5%)
  between operations  14.8 us (2%)
    psum x1, waiting for transfers between devices, axis_by_axis(): half = lax.psum(array, one)  161 us
    psum x1, waiting for transfers between devices, body(): summed = lax.psum(partial_value, 'col')  153 us
    psum x1, waiting for transfers between devices, axis_by_axis(): return lax.psum(half, other)  141 us
    reduce_scatter x1, waiting for transfers between devices, body(): lax.psum_scatter(back_partial, 'row', scatter_dimension=0, tiled=True)  94.2 us
    all_gather x1, waiting for transfers between devices, body(): proj_block = lax.all_gather(projected, 'row', axis=0, tiled=True)  58.8 us
    scatter-add x1, other arithmetic, body(): jax.ops.segment_sum(products, fwd_targets, tile_rows + 1)[:tile_rows]  46 us
    scatter-add x1, other arithmetic, body(): jax.ops.segment_sum(back_products, back_targets, tile_cols + 1)[:tile_cols]  46 us
    dot_general x1, local copies, waits for them, and re-layouts, body(): jnp.einsum('tij,tjf->tif', tile_vals, gathered, preferred_element_type=jn...  23.5 us
  transfers between devices with their start and end apart: 6, of which 5 were waited for; matrix products, arithmetic and copies ran while one was open for 13% of the time, Pallas kernels for 0%

profile of v1, /device:TPU:1, one launch (start us, length us, event | category | flops | bytes accessed | tf_op | source)
XLA Modules:
  0.0 837.8 jit_solution(10920760001872046439)
XLA Ops:
  7.2 0.8 copy-done
  8.0 1.5 convolution_convert_fusion.1
  11.7 0.7 fusion.13
  12.4 58.8 %all-gather.3.cloned.1.call-done = bf16[4096,128]{1,0:T(8,128)(2,1)} async-done(((bf16[256,128]{1,0:T(8,128)(2,1)}), bf16[4096,128]{1,0:T(8,128)(2,1)}) %all-gather.3.cloned.1.call-update) | async-done | bytes 1048592 | tf_op jit(solution)/shard_map/all_gather | solution.py:32
  71.3 12.2 %gather_fusion = bf16[352,128,128]{2,1,0:T(8,128)(2,1)} fusion(bf16[32,128,128]{2,1,0:T(8,128)(2,1)} %bitcast.41, s32[1024]{0:T(1024)S(1)} %pad_clamp_fusion.1), kind=kCustom, calls=%fused_computation | custom fusion | bytes 23070080 | tf_op jit(solution)/shard_map/gather | solution.py:34
  83.5 20.6 %fusion.4 = f32[352,128,128]{1,2,0:T(8,128)} fusion(bf16[352,128,128]{2,1,0:T(8,128)(2,1)} %gather_fusion, bf16[1,1,352,128,128]{4,3,2,1,0:T(8,128)(2,1)} %param.8), kind=kOutput, calls=%fused_computation.8 | convolution fusion | flops 1476395008 | bytes 46137344 | tf_op jit(solution)/shard_map/tij,tjf->tif/dot_general | solution.py:35
  104.1 23.5 %copy.13 = f32[352,128,128]{2,1,0:T(8,128)} copy(f32[352,128,128]{1,2,0:T(8,128)} %fusion.4) | data formatting | bytes 46137344 | tf_op jit(solution)/shard_map/tij,tjf->tif/dot_general | solution.py:35
  127.8 46.0 %scatter_fusion = f32[33,128,128]{2,1,0:T(8,128)S(1)} fusion(f32[33,128,128]{2,1,0:T(8,128)S(1)} %broadcast.191.clone, s32[352]{0:T(512)S(1)} %get-tuple-element.10, f32[352,128,128]{2,1,0:T(8,128)} %copy.13), kind=kCustom, calls=%fused_computation.2 | custom fusion | flops 5767168 | bytes 69207424 | tf_op jit(solution)/shard_map/scatter-add | solution.py:37
  173.9 1.5 slice.12
  175.7 153.0 %all-reduce.4.cloned.1.call-done = f32[4096,128]{1,0:T(8,128)} async-done(((f32[4096,128]{1,0:T(8,128)}), f32[4096,128]{1,0:T(8,128)}) %all-reduce.4.cloned.1.call-update) | async-done | bytes 2097168 | tf_op jit(solution)/shard_map/psum | solution.py:40
  328.6 2.6 multiply_convert_fusion
  331.3 11.0 %gather_fusion.1 = bf16[352,128,128]{2,1,0:T(8,128)(2,1)} fusion(bf16[32,128,128]{2,1,0:T(8,128)(2,1)S(1)} %bitcast.40, s32[1024]{0:T(1024)S(1)} %pad_clamp_fusion), kind=kCustom, calls=%fused_computation.1 | custom fusion | bytes 23070080 | tf_op jit(solution)/shard_map/gather | solution.py:45
  342.3 14.4 %fusion.7 = f32[352,128,128]{1,2,0:T(8,128)} fusion(bf16[352,128,128]{2,1,0:T(8,128)(2,1)} %gather_fusion.1, bf16[1,1,352,128,128]{4,3,2,1,0:T(8,128)(2,1)} %param.8), kind=kOutput, calls=%fused_computation.9 | convolution fusion | flops 1476395008 | bytes 46137344 | tf_op jit(solution)/shard_map/tji,tjf->tif/dot_general | solution.py:46
  356.7 23.5 %copy.15 = f32[352,128,128]{2,1,0:T(8,128)} copy(f32[352,128,128]{1,2,0:T(8,128)} %fusion.7) | data formatting | bytes 46137344 | tf_op jit(solution)/shard_map/tji,tjf->tif/dot_general | solution.py:46
  380.4 46.0 %scatter_fusion.1 = f32[33,128,128]{2,1,0:T(8,128)S(1)} fusion(f32[33,128,128]{2,1,0:T(8,128)S(1)} %broadcast.191, s32[352]{0:T(512)S(1)} %get-tuple-element.11, f32[352,128,128]{2,1,0:T(8,128)} %copy.15), kind=kCustom, calls=%fused_computation.3 | custom fusion | flops 5767168 | bytes 69207424 | tf_op jit(solution)/shard_map/scatter-add | solution.py:50
  426.4 1.5 slice.13
  428.0 94.2 %reduce-scatter.2.cloned.1.call-done = f32[256,128]{1,0:T(8,128)} async-done(((f32[4096,128]{1,0:T(8,128)}), f32[256,128]{1,0:T(8,128)}) %reduce-scatter.2.cloned.1.call-update) | async-done | bytes 131088 | tf_op jit(solution)/shard_map/reduce_scatter | solution.py:53
  522.2 1.7 convolution_bitcast_fusion
  524.0 1.6 multiply_convert_fusion.1
  525.6 161.4 %all-reduce.6.cloned.1.call-done = f32[128,128]{0,1:T(8,128)} async-done(((f32[128,128]{0,1:T(8,128)}), f32[128,128]{0,1:T(8,128)}) %all-reduce.6.cloned.1.call-update) | async-done | bytes 65552 | tf_op jit(solution)/shard_map/psum | solution.py:9
  687.1 1.7 convolution_convert_fusion
  688.8 140.6 %all-reduce.8.cloned.1.call-done = f32[128,128]{0,1:T(8,128)} async-done(((f32[128,128]{0,1:T(8,128)}), f32[128,128]{0,1:T(8,128)}) %all-reduce.8.cloned.1.call-update) | async-done | bytes 65552 | tf_op jit(solution)/shard_map/psum | solution.py:10
  829.4 0.8 broadcast_multiply_fusion
  830.2 0.7 copy.16
  (21 shorter events, 2.4 us)
Async XLA Ops:
  7.2 0.8 copy-start
  7.2 64.1 %all-gather.3.cloned.1.call-start = ((), (), s32[]{:S(2)}) async-start(), calls=%async_computation.1 | async-start | bytes 1114112 | tf_op jit(solution)/shard_map/all_gather | solution.py:32
  9.6 166.1 %all-gather.5.cloned.1.call-start = ((), (), s32[]{:S(2)}) async-start(), calls=%async_computation.3 | async-start | bytes 1114112 | tf_op jit(solution)/shard_map/all_gather | solution.py:43
  10.3 318.3 %all-reduce.4.cloned.1.call-start = ((), (), s32[]{:S(2)}) async-start(), calls=%async_computation.2 | async-start | bytes 4194304 | tf_op jit(solution)/shard_map/psum | solution.py:40
  175.4 346.8 %reduce-scatter.2.cloned.1.call-start = ((), (), s32[]{:S(2)}) async-start(), calls=%async_computation.4 | async-start | bytes 2228224 | tf_op jit(solution)/shard_map/reduce_scatter | solution.py:53
  380.4 306.6 %copy-start.1 = (bf16[128,128]{1,0:T(8,128)(2,1)S(1)}, bf16[128,128]{1,0:T(8,128)(2,1)}, u32[]{:S(2)}) copy-start(bf16[128,128]{1,0:T(8,128)(2,1)} %param.7) | copy-start | bytes 98308
  428.0 259.1 %all-reduce.6.cloned.1.call-start = ((), (), s32[]{:S(2)}) async-start(), calls=%async_computation.5 | async-start | bytes 131072 | tf_op jit(solution)/shard_map/psum | solution.py:9
  523.9 305.4 %all-reduce.8.cloned.1.call-start = ((), (), s32[]{:S(2)}) async-start(), calls=%async_computation.6 | async-start | bytes 131072 | tf_op jit(solution)/shard_map/psum | solution.py:10
Sparse Core Ops, SparseCore 0:
  11.3 59.9 all-gather.2
  73.1 65.9 all-gather.4
  175.5 153.0 all-reduce.3
  428.1 94.0 reduce-scatter.1
  525.2 161.7 all-reduce.5
  689.7 139.6 all-reduce.7
